TPU v7x, 32 devices: a whole 2x2x4 slice. The times are simulated.
32 devices in a mesh: cls: 4 (over y, x), row: 8 (over z, core).
Axes of the slice: x: 2, y: 2, z: 4, core: 2. Of those that a mesh axis runs over, the one named last changes fastest.
Arguments:
- codes: int32 [2048, 1024], P('row'), may hold values from 0 to 63
- split_feature: int32 [16, 7], P('cls'), may hold values from 0 to 1023
- split_bin: int32 [16, 7], P('cls'), may hold values from 0 to 62
- labels: int32 [2048], P('row'), may hold values from 0 to 15
- margins: float32 [2048, 16], P('row', 'cls'), may hold values from -11 to 11
Outputs:
- best_gain: float32 [16, 4], P('cls')
- leaf_value: float32 [16, 8], P('cls')
- grad_next: float32 [2048, 16], P('row', 'cls')
- hess_next: float32 [2048, 16], P('row', 'cls')
All inputs are finite; a program needn't handle non-finite values.
Results may differ from a plain program's by a relative error of at most 0.0013.
Values may be sent and summed in bfloat16 or wider, within the bound.
A program may use at most 64 MiB of HBM per device.

v0:
```python
import jax
import jax.numpy as jnp
from jax import lax
from jax.sharding import PartitionSpec as P

BINS = 64


reg_weight = 1.0
shrink_rate = 0.3


def largest_divisor(total, limit):
    return max(
        (candidate for candidate in range(1, min(total, limit) + 1) if total % candidate == 0)
    )


def lookup(table, node_index):
    hit = node_index[:, :, None] == jnp.arange(table.shape[1], dtype=jnp.int32)[None, None, :]
    return jnp.sum(jnp.where(hit, table[None], jnp.zeros((), table.dtype)), axis=-1)


def node_sums(weights_rows, code_rows):
    width = code_rows.shape[1]
    onehot = (code_rows[:, :, None] == jnp.arange(BINS, dtype=jnp.int32)[None, None, :]).astype(
        jnp.bfloat16
    )
    onehot = onehot.reshape(code_rows.shape[0], width * BINS)
    return jnp.dot(weights_rows, onehot, preferred_element_type=jnp.float32)


def local(codes, split_feature, split_bin, labels, margins):
    local_rows = codes.shape[0]
    features = codes.shape[1]
    classes = margins.shape[1]
    nodes = (split_feature.shape[1] + 1) // 2
    levels = nodes.bit_length() - 1
    row_devices = lax.axis_size("row")
    owned = features // row_devices
    stat_count = 2 * classes * nodes
    class_ids = lax.axis_index("cls") * classes + jnp.arange(classes, dtype=jnp.int32)
    target = (labels[:, None] == class_ids[None, :]).astype(jnp.float32)
    expon = jnp.exp(margins)
    totals = lax.psum(jnp.sum(expon, axis=1), "cls")
    probab = expon / totals[:, None]
    grad_low = (probab - target).astype(jnp.bfloat16)
    hess_low = (2.0 * probab * (1.0 - probab)).astype(jnp.bfloat16)
    node_index = jnp.zeros((local_rows, classes), jnp.int32)
    for level in range(levels):
        code_here = jnp.take_along_axis(codes, lookup(split_feature, node_index), axis=1)
        node_index = jnp.where(
            code_here <= lookup(split_bin, node_index), 2 * node_index + 1, 2 * node_index + 2
        )
    local_node = node_index - (nodes - 1)
    member = local_node[:, :, None] == jnp.arange(nodes, dtype=jnp.int32)[None, None, :]
    stacked = jnp.stack([grad_low, hess_low])
    weights_rows = (stacked[:, :, :, None] * member[None].astype(jnp.bfloat16)).transpose(
        0, 2, 3, 1
    )
    weights_rows = weights_rows.reshape(stat_count, local_rows)
    width = largest_divisor(lax.axis_size("row") * owned, 64)

    def one_block(index):
        sub_codes = lax.dynamic_slice_in_dim(codes, index * width, width, 1)
        result = node_sums(weights_rows, sub_codes).reshape(stat_count, width, BINS)
        return result.transpose(1, 0, 2).reshape(width, stat_count * BINS)

    blocks = lax.map(one_block, jnp.arange(lax.axis_size("row") * owned // width, dtype=jnp.int32))
    owned_hist = lax.psum_scatter(
        blocks.reshape(lax.axis_size("row") * owned, stat_count * BINS),
        "row",
        scatter_dimension=0,
        tiled=True,
    )
    hist_five = owned_hist.reshape(owned, 2, classes, nodes, BINS)
    cumul = jnp.cumsum(hist_five, axis=-1)
    g_left = cumul[:, 0, :, :, :-1]
    h_left = cumul[:, 1, :, :, :-1]
    g_all = cumul[:, 0, :, :, -1:]
    h_all = cumul[:, 1, :, :, -1:]
    gain = (
        g_left * g_left / (h_left + reg_weight)
        + (g_all - g_left) ** 2 / (h_all - h_left + reg_weight)
        - g_all * g_all / (h_all + reg_weight)
    )
    local_best = jnp.max(gain / (h_all + reg_weight), axis=(0, 3))
    best_gain = lax.pmax(local_best, "row")
    leaf_feat = split_feature[:, nodes - 1 :]
    leaf_bin = split_bin[:, nodes - 1 :]
    final_feat = lookup(split_feature, node_index)
    code_last = jnp.take_along_axis(codes, final_feat, axis=1)
    side = (code_last > lookup(split_bin, node_index)).astype(jnp.int32)
    base = lax.axis_index("row") * owned
    fsel = (
        leaf_feat[None, :, :] - base == jnp.arange(owned, dtype=jnp.int32)[:, None, None]
    ).astype(jnp.float32)
    chosen = jnp.sum(hist_five * fsel[:, None, :, :, None], axis=0)
    below = (jnp.arange(BINS, dtype=jnp.int32)[None, None, :] <= leaf_bin[:, :, None]).astype(
        jnp.float32
    )
    left_part = jnp.sum(chosen * below[None], axis=-1)
    right_part = jnp.sum(chosen * (1.0 - below[None]), axis=-1)
    left_sum, right_sum = lax.psum((left_part, right_part), "row")
    left_value = -shrink_rate * left_sum[0] / (left_sum[1] + reg_weight)
    right_value = -shrink_rate * right_sum[0] / (right_sum[1] + reg_weight)
    leaf_value = jnp.stack([left_value, right_value], axis=-1).reshape(classes, 2 * nodes)
    leaf_index = 2 * local_node + side
    update = lookup(leaf_value, leaf_index)
    updated = margins + update
    expon_next = jnp.exp(updated)
    totals_next = lax.psum(jnp.sum(expon_next, axis=1), "cls")
    probab_next = expon_next / totals_next[:, None]
    grad_next = probab_next - target
    hess_next = 2.0 * probab_next * (1.0 - probab_next)
    return (best_gain, leaf_value, grad_next, hess_next)


def solution(mesh):
    in_specs = (P("row", None), P("cls", None), P("cls", None), P("row"), P("row", "cls"))
    out_specs = (P("cls", None), P("cls", None), P("row", "cls"), P("row", "cls"))
    return jax.shard_map(local, mesh=mesh, in_specs=in_specs, out_specs=out_specs, check_vma=False)
```

profile of v0, /device:TPU:0, one launch (start us, length us, event | category | flops | bytes accessed | tf_op | source)
XLA Modules:
  0.0 276.3 jit_solution(9787670139737409248)
XLA Ops:
  9.2 2.6 copy.46
  11.9 8.6 %gather_fusion = s32[1024]{0:T(1024)S(1)} fusion(s32[256,1024]{1,0:T(8,128)S(1)} %copy-done, s32[1024]{0:T(1024)S(1)} %reshape.193), kind=kCustom, calls=%fused_computation.clone | custom fusion | bytes 16384 | tf_op jit(solution)/shard_map/jit(take_along_axis)/gather | solution.py:51
  21.1 8.6 %gather_fusion.1 = s32[1024]{0:T(1024)S(1)} fusion(s32[256,1024]{1,0:T(8,128)S(1)} %copy-done, s32[1024]{0:T(1024)S(1)} %reshape.198), kind=kCustom, calls=%fused_computation.1.clone | custom fusion | bytes 16384 | tf_op jit(solution)/shard_map/jit(take_along_axis)/gather | solution.py:51
  30.0 11.4 %psum.28 = f32[256]{0:T(256)S(1)} all-reduce(f32[256]{0:T(256)S(1)} %exponential_reduce_fusion), channel_id=1, replica_groups=mesh['cls'=4,'row'=8] {'cls'}, use_global_device_ids=true, to_apply=%region_1.0 | all-reduce | flops 256 | bytes 2048 | tf_op jit(solution)/shard_map/psum | solution.py:45
  41.4 94.7 %while.11 = (s32[]{:T(128)}, f32[16,64,2048]{2,1,0:T(8,128)}, s32[16]{0:T(128)S(1)}, s32[256,1024]{0,1:T(8,128)}, bf16[4,4,256]{2,1,0:T(4,128)(2,1)S(1)}, /*inde...) while((s32[]{:T(128)}, f32[16,64,2048]{2,1,0:T(8,128)}, ...), condition=%wide.region_7.9_spmd.clone, body=%wide.region_6.8_spmd.clone.sunk | while | flops 68165640 | bytes 7156387 | solution.py:69
  42.7 0.8 constant_dynamic-slice_fusion.2
  48.6 0.8 constant_dynamic-slice_fusion.2
  52.4 0.9 constant_dynamic-update-slice_fusion.2
  54.5 0.8 constant_dynamic-slice_fusion.2
  58.4 0.9 constant_dynamic-update-slice_fusion.2
  64.3 0.9 constant_dynamic-update-slice_fusion.2
  76.1 0.9 constant_dynamic-update-slice_fusion.2
  87.9 0.9 constant_dynamic-update-slice_fusion.2
  99.8 0.9 constant_dynamic-update-slice_fusion.2
  111.6 0.9 constant_dynamic-update-slice_fusion.2
  123.5 0.9 constant_dynamic-update-slice_fusion.2
  135.3 0.9 constant_dynamic-update-slice_fusion.2
  137.8 8.6 %gather_fusion.2 = s32[1024]{0:T(1024)S(1)} fusion(s32[256,1024]{1,0:T(8,128)S(1)} %copy-done, s32[1024]{0:T(1024)S(1)} %reshape.203), kind=kCustom, calls=%fused_computation.2.clone | custom fusion | bytes 16384 | tf_op jit(solution)/shard_map/jit(take_along_axis)/gather | solution.py:92
  146.8 78.5 %reduce-scatter.2.cloned.1.call-done = f32[128,2048]{1,0:T(8,128)} async-done(((f32[1024,2048]{1,0:T(8,128)}), f32[128,2048]{1,0:T(8,128)}) %reduce-scatter.2.cloned.1.call-update) | async-done | bytes 1048592 | tf_op jit(solution)/shard_map/reduce_scatter | solution.py:70
  225.3 1.5 copy.47
  227.6 1.4 multiply_reduce_fusion
  229.2 13.9 %all-reduce = (f32[2,4,4]{2,1,0:T(4,128)S(1)}, f32[2,4,4]{2,1,0:T(4,128)S(1)}) all-reduce(f32[2,4,4]{2,1,0:T(4,128)S(1)} %get-tuple-element.84, f32[2,4,4]{2,1,0:T(4,128)S(1)} %get-tuple-element.83), channel_id=1, replica_groups=mesh['cls'=4,'row'=8] {'row'}, use_global_device_ids=true, to_apply=%region_16.18 | all-reduce | flops 64 | bytes 512 | tf_op jit(solution)/shard_map/psum | solution.py:104
  243.4 10.0 %psum.31 = f32[256]{0:T(256)S(1)} all-reduce(f32[256]{0:T(256)S(1)} %fusion.16), channel_id=1, replica_groups=mesh['cls'=4,'row'=8] {'cls'}, use_global_device_ids=true, to_apply=%region_21.23 | all-reduce | flops 256 | bytes 2048 | tf_op jit(solution)/shard_map/psum | solution.py:112
  255.3 14.1 %pmax.7 = f32[4,4]{1,0:T(4,128)} all-reduce(f32[4,4]{1,0:T(4,128)S(1)} %fusion.4), channel_id=1, replica_groups=mesh['cls'=4,'row'=8] {'row'}, use_global_device_ids=true, to_apply=%region_11.13 | all-reduce | flops 16 | bytes 128 | tf_op jit(solution)/shard_map/pmax | solution.py:88
  (246 shorter events, 81.4 us)
Async XLA Ops:
  7.2 4.7 %copy-start = (s32[256,1024]{1,0:T(8,128)S(1)}, s32[256,1024]{1,0:T(8,128)}, u32[]{:S(2)}) copy-start(s32[256,1024]{1,0:T(8,128)} %param.9) | copy-start | bytes 3145732
  7.2 218.1 %reduce-scatter.2.cloned.1.call-start = ((), (), s32[]{:S(2)}) async-start(), calls=%async_computation.1 | async-start | bytes 9437184 | tf_op jit(solution)/shard_map/reduce_scatter | solution.py:70
  21.1 8.9 %copy-start.1 = (f32[256,4]{0,1:T(4,128)S(1)}, f32[256,4]{0,1:T(4,128)}, u32[]{:S(2)}) copy-start(f32[256,4]{0,1:T(4,128)} %param.13) | copy-start | bytes 12292
  21.1 20.3 %copy-start.5 = (s32[256]{0:T(256)S(1)}, s32[256]{0:T(256)}, u32[]{:S(2)}) copy-start(s32[256]{0:T(256)} %param.12) | copy-start | bytes 3076
  136.1 0.7 copy-start.3
  136.1 0.8 copy-start.4
  243.3 26.1 %copy-start.2 = (f32[4,8]{1,0:T(4,128)}, f32[4,8]{1,0:T(4,128)S(1)}, u32[]{:S(2)}) copy-start(f32[4,8]{1,0:T(4,128)S(1)} %copy.56) | copy-start | bytes 388
Sparse Core Ops, SparseCore 0:
  136.3 88.9 reduce-scatter.1
where the time goes:
time: 278 us; the launch traced here: 276 us
  local copies, waits for them, and re-layouts  94.6 us (34%)
  waiting for transfers between devices  78.5 us (28%)
  blocking collectives  49.4 us (18%)
  other arithmetic  16.6 us (6%)
  between operations  14.3 us (5%)
  matrix products  11.6 us (4%)
  loops' own time  11.1 us (4%)
    reduce_scatter x1, waiting for transfers between devices, local(): lax.psum_scatter(blocks.reshape(lax.axis_size('row') * owned, stat_count...  78.5 us
    gather x10, local copies, waits for them, and re-layouts, local(): jnp.take_along_axis(codes, lookup(split_feature, node_index), axis=1)  18.1 us
    pmax x1, blocking collectives, local(): best_gain = lax.pmax(local_best, 'row')  14.1 us
    psum x1, blocking collectives, local(): left_sum, right_sum = lax.psum((left_part, right_part), 'row')  13.9 us
    dynamic_slice x16, local copies, waits for them, and re-layouts, one_block(): sub_codes = lax.dynamic_slice_in_dim(codes, index * width, width, 1)  13.6 us
    dynamic_update_slice x16, local copies, waits for them, and re-layouts, local(): lax.map(one_block, jnp.arange(lax.axis_size('row') * owned // width, dtyp...  13.5 us
    dot_general x16, matrix products, node_sums(): return jnp.dot(weights_rows, onehot, preferred_element_type=jnp.float32)  11.6 us
    eq x16, other arithmetic, node_sums(): code_rows[:, :, None] == jnp.arange(BINS, dtype=jnp.int32)[None, None, :]  11.4 us
  transfers between devices with their start and end apart: 1, of which 1 were waited for; matrix products, arithmetic and copies ran while one was open for 4% of the time, Pallas kernels for 0%

commit v1 on v0

v1 whole, which is shorter than its diff:
```python
import functools
import jax
import jax.numpy as jnp
from jax import lax
from jax.experimental import pallas as pl
from jax.experimental.pallas import tpu as pltpu
from jax.sharding import PartitionSpec as P

BINS = 64
REG = 1.0
SHRINK = 0.3
MESH = pl.DeviceIdType.MESH


def kernel(dims, codes_ref, sf_ref, sb_ref, lab_ref, mar_ref, bg_ref, lv_ref, gn_ref, hn_ref,
           sel, picked, csend, crecv, blocks, marg, tags, codef, wts, le, nextg, nexth,
           gsend, grecv, hsend, hrecv,
           row_s, row_r, cls_s, cls_r, cod_s, cod_r, g_s, g_r, h_s, h_r):
    nc, nr, C, Rl, F, NT, chunk = dims
    CT, R = C * nc, Rl * nr
    nodes = (NT + 1) // 2
    leaves = 2 * nodes
    levels = nodes.bit_length() - 1
    fq = F // nc
    fb = fq // nr
    f32, bf16 = jnp.float32, jnp.bfloat16
    c = lax.axis_index("cls")
    r = lax.axis_index("row")

    def row_peer(k):
        return (c, lax.rem(r + k, nr))

    def cls_peer(k):
        return (lax.rem(c + k, nc), r)

    barrier = pltpu.get_barrier_semaphore()
    for k in range(1, nr):
        pl.semaphore_signal(barrier, inc=1, device_id=row_peer(k), device_id_type=MESH)
    for k in range(1, nc):
        pl.semaphore_signal(barrier, inc=1, device_id=cls_peer(k), device_id_type=MESH)

    lane = lax.broadcasted_iota(jnp.int32, (C, F), 1)
    sel[...] = jnp.zeros_like(sel)
    for n in range(NT):
        sel[n * C:(n + 1) * C, :] = jnp.where(lane == sf_ref[:, n:n + 1], 1.0, 0.0).astype(f32)
    low = codes_ref[...].astype(f32).astype(bf16)
    picked[...] = lax.dot_general(sel[...].astype(bf16), low, (((1,), (1,)), ((), ())),
                                  preferred_element_type=f32)
    bins = sb_ref[...].astype(f32)
    at = jnp.zeros((C, Rl), jnp.int32)
    for level in range(levels + 1):
        first = 2 ** level - 1
        code = picked[first * C:(first + 1) * C, :]
        cut = jnp.broadcast_to(bins[:, first:first + 1], (C, Rl))
        for j in range(1, 2 ** level):
            n = first + j
            hit = at == j
            code = jnp.where(hit, picked[n * C:(n + 1) * C, :], code)
            cut = jnp.where(hit, bins[:, n:n + 1], cut)
        at = 2 * at + jnp.where(code > cut, 1, 0)
    ids = c * C + lax.broadcasted_iota(jnp.int32, (C, Rl), 0)
    tag = at.astype(f32) + jnp.where(lab_ref[...] == ids, float(leaves), 0.0)
    blocks[c, r, 0:C, :] = mar_ref[...]
    blocks[c, r, C:2 * C, :] = tag

    pl.semaphore_wait(barrier, nr - 1 + nc - 1)

    def row_copy(k):
        return pltpu.make_async_remote_copy(
            src_ref=blocks.at[c, r], dst_ref=blocks.at[c, r], send_sem=row_s.at[k],
            recv_sem=row_r.at[k], device_id=row_peer(k), device_id_type=MESH)

    def cls_copy(k):
        return pltpu.make_async_remote_copy(
            src_ref=blocks.at[c], dst_ref=blocks.at[c], send_sem=cls_s.at[k],
            recv_sem=cls_r.at[k], device_id=cls_peer(k), device_id_type=MESH)

    def cod_copy(k):
        return pltpu.make_async_remote_copy(
            src_ref=csend.at[lax.rem(r + k, nr)], dst_ref=crecv.at[r], send_sem=cod_s.at[k],
            recv_sem=cod_r.at[k], device_id=row_peer(k), device_id_type=MESH)

    rows = [row_copy(k) for k in range(1, nr)]
    for d in rows:
        d.start()

    quarter = codes_ref[:, pl.ds(pl.multiple_of(c * fq, 128), fq)].astype(f32)
    turned = quarter.T.astype(bf16)
    for j in range(nr):
        csend[j] = turned[j * fb:(j + 1) * fb, :]
    cods = [cod_copy(k) for k in range(1, nr)]
    for d in cods:
        d.start()
    crecv[r] = csend[r]

    for d in rows:
        d.wait_recv()
    clss = [cls_copy(k) for k in range(1, nc)]
    for d in clss:
        d.start()
    for d in clss:
        d.wait_recv()

    for a in range(nc):
        for q in range(nr):
            marg[a * C:(a + 1) * C, q * Rl:(q + 1) * Rl] = blocks[a, q, 0:C, :]
            tags[a * C:(a + 1) * C, q * Rl:(q + 1) * Rl] = blocks[a, q, C:2 * C, :]

    expon = jnp.exp(marg[...])
    tag_all = tags[...]
    target = jnp.where(tag_all >= leaves, 1.0, 0.0).astype(f32)
    leaf = tag_all - leaves * target
    probab = expon / jnp.sum(expon, axis=0, keepdims=True)
    grad = (probab - target).astype(bf16).astype(f32)
    hess = (2.0 * probab * (1.0 - probab)).astype(bf16).astype(f32)
    g_leaf, h_leaf = [], []
    for n in range(nodes):
        gn_, hn_ = [], []
        for s in range(2):
            hit = leaf == float(2 * n + s)
            gs = jnp.where(hit, grad, 0.0)
            hs = jnp.where(hit, hess, 0.0)
            gn_.append(gs)
            hn_.append(hs)
            g_leaf.append(jnp.sum(gs, axis=1, keepdims=True))
            h_leaf.append(jnp.sum(hs, axis=1, keepdims=True))
        wts[n * CT:(n + 1) * CT, :] = (gn_[0] + gn_[1]).astype(bf16)
        wts[(nodes + n) * CT:(nodes + n + 1) * CT, :] = (hn_[0] + hn_[1]).astype(bf16)
    values = [-SHRINK * g / (h + REG) for g, h in zip(g_leaf, h_leaf)]
    g_all = [g_leaf[2 * n] + g_leaf[2 * n + 1] for n in range(nodes)]
    h_all = [h_leaf[2 * n] + h_leaf[2 * n + 1] for n in range(nodes)]

    for d in cods:
        d.wait_recv()
    for q in range(nr):
        codef[:, q * Rl:(q + 1) * Rl] = crecv[q].astype(f32)
    above = (lax.broadcasted_iota(jnp.int32, (BINS, R), 0) + 1).astype(f32).astype(bf16)
    zero, one = jnp.zeros((), bf16), jnp.ones((), bf16)
    width = chunk * BINS
    last = lax.rem(lax.broadcasted_iota(jnp.int32, (CT, width), 1), BINS) == BINS - 1
    best = [None] * nodes
    for i in range(fb // chunk):
        for j in range(chunk):
            row = jnp.broadcast_to(codef[i * chunk + j:i * chunk + j + 1, :], (BINS, R)).astype(bf16)
            le[i % 2, j * BINS:(j + 1) * BINS, :] = jnp.clip(above - row, zero, one)
        sums = lax.dot_general(wts[...], le[i % 2], (((1,), (1,)), ((), ())),
                               preferred_element_type=f32)
        for n in range(nodes):
            gl = sums[n * CT:(n + 1) * CT, :]
            hl = sums[(nodes + n) * CT:(nodes + n + 1) * CT, :]
            gr = g_all[n] - gl
            hr = h_all[n] - hl + REG
            hl = hl + REG
            gain = (gl * gl * hr + gr * gr * hl) / (hl * hr)
            gain = jnp.where(last, -jnp.inf, gain)
            best[n] = gain if best[n] is None else jnp.maximum(best[n], gain)

    spot = lax.broadcasted_iota(jnp.int32, (CT, 128), 1)
    tops = jnp.zeros((CT, 128), f32)
    for n in range(nodes):
        top = jnp.max(best[n], axis=1, keepdims=True)
        den = h_all[n] + REG
        top = (top - g_all[n] * g_all[n] / den) / den
        tops = jnp.where(spot == n, top, tops)
    for a in range(nc):
        gsend[a] = tops[a * C:(a + 1) * C, :]

    def g_copy(k):
        return pltpu.make_async_remote_copy(
            src_ref=gsend.at[lax.rem(c + k, nc)], dst_ref=grecv.at[k], send_sem=g_s.at[k],
            recv_sem=g_r.at[k], device_id=cls_peer(k), device_id_type=MESH)

    def h_copy(k):
        return pltpu.make_async_remote_copy(
            src_ref=hsend, dst_ref=hrecv.at[k], send_sem=h_s.at[k],
            recv_sem=h_r.at[k], device_id=row_peer(k), device_id_type=MESH)

    gs_ = [g_copy(k) for k in range(1, nc)]
    for d in gs_:
        d.start()

    here = pl.ds(pl.multiple_of(r * Rl, 128), Rl)
    tag_own = tags[:, here]
    target_own = jnp.where(tag_own >= leaves, 1.0, 0.0).astype(f32)
    leaf_own = tag_own - leaves * target_own
    update = jnp.zeros((CT, Rl), f32)
    for l in range(leaves):
        update = jnp.where(leaf_own == float(l), values[l], update)
    expon2 = jnp.exp(marg[:, here] + update)
    prob2 = expon2 / jnp.sum(expon2, axis=0, keepdims=True)
    gnext = prob2 - target_own
    hnext = 2.0 * prob2 * (1.0 - prob2)
    spot2 = lax.broadcasted_iota(jnp.int32, (CT, 128), 1)
    val = jnp.zeros((CT, 128), f32)
    for l in range(leaves):
        val = jnp.where(spot2 == l, values[l], val)
    for a in range(nc):
        nextg[a, :, 0:Rl] = gnext[a * C:(a + 1) * C, :]
        nextg[a, :, Rl:Rl + 128] = val[a * C:(a + 1) * C, :]
        nexth[a] = hnext[a * C:(a + 1) * C, :]
    gn_ref[...] = nextg[c, :, 0:Rl]
    hn_ref[...] = nexth[c]
    lv_ref[...] = nextg[c, :, Rl:Rl + leaves]

    top = gsend[c]
    for k in range(1, nc):
        gs_[k - 1].wait_recv()
        top = jnp.maximum(top, grecv[k])
    hsend[...] = top
    hs_ = [h_copy(k) for k in range(1, nr)]
    for d in hs_:
        d.start()
    for k in range(1, nr):
        hs_[k - 1].wait_recv()
        top = jnp.maximum(top, hrecv[k])
    bg_ref[...] = top[:, 0:nodes]
    for d in rows + clss + cods + gs_ + hs_:
        d.wait_send()


def local(codes, split_feature, split_bin, labels, margins):
    Rl, F = codes.shape
    C, NT = split_feature.shape
    nc, nr = lax.axis_size("cls"), lax.axis_size("row")
    nodes = (NT + 1) // 2
    CT, R = C * nc, Rl * nr
    fb = F // (nc * nr)
    chunk = min(4, fb)
    f32, bf16 = jnp.float32, jnp.bfloat16
    pad = -(-NT * C // 16) * 16
    dma = pltpu.SemaphoreType.DMA
    vmem = pl.BlockSpec(memory_space=pltpu.VMEM)
    best, leaf, grad, hess = pl.pallas_call(
        functools.partial(kernel, (nc, nr, C, Rl, F, NT, chunk)),
        out_shape=(jax.ShapeDtypeStruct((C, nodes), f32), jax.ShapeDtypeStruct((C, 2 * nodes), f32),
                   jax.ShapeDtypeStruct((C, Rl), f32), jax.ShapeDtypeStruct((C, Rl), f32)),
        in_specs=[vmem] * 5,
        out_specs=(vmem,) * 4,
        scratch_shapes=[
            pltpu.VMEM((pad, F), f32), pltpu.VMEM((pad, Rl), f32),
            pltpu.VMEM((nr, fb, Rl), bf16), pltpu.VMEM((nr, fb, Rl), bf16),
            pltpu.VMEM((nc, nr, 2 * C, Rl), f32),
            pltpu.VMEM((CT, R), f32), pltpu.VMEM((CT, R), f32),
            pltpu.VMEM((fb, R), f32), pltpu.VMEM((2 * nodes * CT, R), bf16),
            pltpu.VMEM((2, chunk * BINS, R), bf16),
            pltpu.VMEM((nc, C, Rl + 128), f32), pltpu.VMEM((nc, C, Rl), f32),
            pltpu.VMEM((nc, C, 128), f32), pltpu.VMEM((nc, C, 128), f32),
            pltpu.VMEM((C, 128), f32), pltpu.VMEM((nr, C, 128), f32),
            dma((nr,)), dma((nr,)), dma((nc,)), dma((nc,)), dma((nr,)), dma((nr,)),
            dma((nc,)), dma((nc,)), dma((nr,)), dma((nr,)),
        ],
        compiler_params=pltpu.CompilerParams(
            collective_id=0, has_side_effects=True, vmem_limit_bytes=48 * 2 ** 20),
        name="boost",
    )(codes, split_feature, split_bin, labels.reshape(1, Rl), margins.T)
    return best, leaf, grad.T, hess.T


def solution(mesh):
    in_specs = (P("row", None), P("cls", None), P("cls", None), P("row"), P("row", "cls"))
    out_specs = (P("cls", None), P("cls", None), P("row", "cls"), P("row", "cls"))
    return jax.shard_map(local, mesh=mesh, in_specs=in_specs, out_specs=out_specs, check_vma=False)
```

time: 278 us -> 31.8 us (0.11)
  local copies, waits for them, and re-layouts: 94.6 us -> 5.61 us
  waiting for transfers between devices: 78.5 us -> 0 us
  blocking collectives: 49.4 us -> 0 us
  Pallas kernels: 0 us -> 25.2 us
  other arithmetic: 16.6 us -> 0 us
  between operations: 14.3 us -> 0.66 us
  matrix products: 11.6 us -> 0 us
  loops' own time: 11.1 us -> 0 us
    reduce_scatter x1 -> x0, waiting for transfers between devices: 78.5 us -> none  [local(): lax.psum_scatter(blocks.reshape(lax.axis_size('row') * owned, stat_count...]
    psum x3 -> x0, blocking collectives: 35.3 us -> none  [the longest x1 13.9 us: local(): left_sum, right_sum = lax.psum((left_part, right_part), 'row')]
    gather x15 -> x0, local copies, waits for them, and re-layouts: 27.1 us -> none  [the longest x10 18.1 us: local(): jnp.take_along_axis(codes, lookup(split_feature, node_index), axis=1)]
    pallas_call x0 -> x1, Pallas kernels: none -> 25.2 us  [local(): pl.pallas_call(functools.partial(kernel, (nc, nr, C, Rl, F, NT, chunk)),...]
    dynamic_slice x32 -> x0, local copies, waits for them, and re-layouts: 22.9 us -> none  [the longest x16 13.6 us: one_block(): sub_codes = lax.dynamic_slice_in_dim(codes, index * width, width, 1)]
    pmax x1 -> x0, blocking collectives: 14.1 us -> none  [local(): best_gain = lax.pmax(local_best, 'row')]
    dynamic_update_slice x16 -> x0, local copies, waits for them, and re-layouts: 13.5 us -> none  [local(): lax.map(one_block, jnp.arange(lax.axis_size('row') * owned // width, dtyp...]
    dot_general x16 -> x0, matrix products: 11.6 us -> none  [node_sums(): return jnp.dot(weights_rows, onehot, preferred_element_type=jnp.float32)]
  transfers between devices with their start and end apart: 1 -> 0, of which waited for: 1 -> 0; matrix products, arithmetic and copies ran while one was open for 4% -> 0% of each run, Pallas kernels for 0% -> 0%
where the time goes in v1:
time: 31.8 us; the launch traced here: 31.5 us
  Pallas kernels  25.2 us (79%)
  local copies, waits for them, and re-layouts  5.61 us (18%)
  between operations  0.66 us (2%)
    pallas_call x1, Pallas kernels, local(): pl.pallas_call(functools.partial(kernel, (nc, nr, C, Rl, F, NT, chunk)),...  25.2 us
    unnamed x14, local copies, waits for them, and re-layouts  5.61 us

profile of v1, /device:TPU:0, one launch (start us, length us, event | category | flops | bytes accessed | tf_op | source)
XLA Modules:
  0.0 31.5 jit_solution(6126400259497770473)
XLA Ops:
  0.6 0.0 copy-start.2
  0.6 0.0 copy-start.4
  0.7 0.7 %copy-done.2 = s32[4,7]{1,0:T(4,128)S(1)} copy-done((s32[4,7]{1,0:T(4,128)S(1)}, s32[4,7]{1,0:T(4,128)}, u32[]{:S(2)}) %copy-start.2) | copy-done | bytes 136
  1.3 0.0 copy-done.4
  1.3 0.0 copy-start
  1.3 1.2 %copy-done = s32[256,1024]{1,0:T(8,128)S(1)} copy-done((s32[256,1024]{1,0:T(8,128)S(1)}, s32[256,1024]{1,0:T(8,128)}, u32[]{:S(2)}) %copy-start) | copy-done | bytes 1048600
  2.6 0.0 copy-start.1
  2.6 0.7 %copy-done.1 = f32[256,4]{0,1:T(4,128)S(1)} copy-done((f32[256,4]{0,1:T(4,128)S(1)}, f32[256,4]{0,1:T(4,128)}, u32[]{:S(2)}) %copy-start.1) | copy-done | bytes 4120
  3.2 0.0 copy-start.3
  3.2 0.7 %copy-done.3 = s32[4,7]{1,0:T(4,128)S(1)} copy-done((s32[4,7]{1,0:T(4,128)S(1)}, s32[4,7]{1,0:T(4,128)}, u32[]{:S(2)}) %copy-start.3) | copy-done | bytes 136
  3.9 25.2 %boost.1 = (f32[4,4]{1,0:T(4,128)S(1)}, f32[4,8]{1,0:T(4,128)S(1)}, f32[4,256]{1,0:T(4,128)S(1)}, f32[4,256]{1,0:T(4,128)S(1)}) custom-call(s32[256,1024]{1,0:T(8,128)S(1)} %copy-done, s32[4,7]{1,0:T(4,128)S(1)} %copy-done.2, s32[4,7]{1,0:T(4,128)S(1)} %copy-done.3, s32[1,256]{1,0:T(1,128)S(1)} %bitcast.7, f32[4,256]{1,0:T(4,128)S(1)} %bitcast.4), custom_call_target="tpu_custom_call" | custom-call | tf_op jit(solution)/shard_map/boost/pallas_call | solution.py:233
  29.2 0.6 %copy.13 = f32[4,4]{1,0:T(4,128)} copy(f32[4,4]{1,0:T(4,128)S(1)} %get-tuple-element.16) | data formatting | bytes 128
  29.8 0.6 %copy.14 = f32[4,8]{1,0:T(4,128)} copy(f32[4,8]{1,0:T(4,128)S(1)} %get-tuple-element.17) | data formatting | bytes 256
  30.3 0.6 %copy.15 = f32[256,4]{0,1:T(4,128)} copy(f32[256,4]{0,1:T(4,128)S(1)} %bitcast.6) | data formatting | bytes 8192
  30.9 0.6 %copy.16 = f32[256,4]{0,1:T(4,128)} copy(f32[256,4]{0,1:T(4,128)S(1)} %bitcast.5) | data formatting | bytes 8192
Async XLA Ops:
  0.6 0.7 %copy-start.2 = (s32[4,7]{1,0:T(4,128)S(1)}, s32[4,7]{1,0:T(4,128)}, u32[]{:S(2)}) copy-start(s32[4,7]{1,0:T(4,128)} %sf_ref.1) | copy-start | bytes 340
  0.6 0.7 %copy-start.4 = (s32[256]{0:T(256)S(1)}, s32[256]{0:T(256)}, u32[]{:S(2)}) copy-start(s32[256]{0:T(256)} %param.8) | copy-start | bytes 3076
  1.3 1.2 %copy-start = (s32[256,1024]{1,0:T(8,128)S(1)}, s32[256,1024]{1,0:T(8,128)}, u32[]{:S(2)}) copy-start(s32[256,1024]{1,0:T(8,128)} %codes_ref.1) | copy-start | bytes 3145732
  2.6 0.7 %copy-start.1 = (f32[256,4]{0,1:T(4,128)S(1)}, f32[256,4]{0,1:T(4,128)}, u32[]{:S(2)}) copy-start(f32[256,4]{0,1:T(4,128)} %param.9) | copy-start | bytes 12292
  3.2 0.7 %copy-start.3 = (s32[4,7]{1,0:T(4,128)S(1)}, s32[4,7]{1,0:T(4,128)}, u32[]{:S(2)}) copy-start(s32[4,7]{1,0:T(4,128)} %sb_ref.1) | copy-start | bytes 340

commit v2 on v1

--- a/solution.py
+++ b/solution.py
@@ -12,10 +12,10 @@
 MESH = pl.DeviceIdType.MESH
 
 
-def kernel(dims, codes_ref, sf_ref, sb_ref, lab_ref, mar_ref, bg_ref, lv_ref, gn_ref, hn_ref,
-           sel, picked, csend, crecv, blocks, marg, tags, codef, wts, le, nextg, nexth,
-           gsend, grecv, hsend, hrecv,
-           row_s, row_r, cls_s, cls_r, cod_s, cod_r, g_s, g_r, h_s, h_r):
+def kernel(dims, codes_in, sf_in, sb_in, lab_in, mar_in, bg_ref, lv_ref, gn_ref, hn_ref,
+           codes_ref, sf_ref, sb_ref, lab_ref, mar_ref, sel, picked, csend, crecv, blocks, marg, tags, wts, le, nextg, nexth,
+           gsend, grecv,
+           in_s, row_s, row_r, cls_s, cls_r, cod_s, cod_r, g_s, g_r):
     nc, nr, C, Rl, F, NT, chunk = dims
     CT, R = C * nc, Rl * nr
     nodes = (NT + 1) // 2
@@ -33,11 +33,19 @@
     def cls_peer(k):
         return (lax.rem(c + k, nc), r)
 
+    def far_peer(kc, kr):
+        return (lax.rem(c + kc, nc), lax.rem(r + kr, nr))
+
+    loads = [pltpu.make_async_copy(src, dst, in_s.at[i]) for i, (src, dst) in enumerate(
+        [(sf_in, sf_ref), (codes_in, codes_ref), (sb_in, sb_ref), (lab_in, lab_ref), (mar_in, mar_ref)])]
+    for d in loads:
+        d.start()
     barrier = pltpu.get_barrier_semaphore()
-    for k in range(1, nr):
-        pl.semaphore_signal(barrier, inc=1, device_id=row_peer(k), device_id_type=MESH)
-    for k in range(1, nc):
-        pl.semaphore_signal(barrier, inc=1, device_id=cls_peer(k), device_id_type=MESH)
+    far = [(kc, kr) for kc in range(nc) for kr in range(nr) if kc + kr > 0]
+    for kc, kr in far:
+        pl.semaphore_signal(barrier, inc=1, device_id=far_peer(kc, kr), device_id_type=MESH)
+    for d in loads:
+        d.wait()
 
     lane = lax.broadcasted_iota(jnp.int32, (C, F), 1)
     sel[...] = jnp.zeros_like(sel)
@@ -63,41 +71,62 @@
     blocks[c, r, 0:C, :] = mar_ref[...]
     blocks[c, r, C:2 * C, :] = tag
 
-    pl.semaphore_wait(barrier, nr - 1 + nc - 1)
+    pl.semaphore_wait(barrier, nc * nr - 1)
 
     def row_copy(k):
         return pltpu.make_async_remote_copy(
             src_ref=blocks.at[c, r], dst_ref=blocks.at[c, r], send_sem=row_s.at[k],
             recv_sem=row_r.at[k], device_id=row_peer(k), device_id_type=MESH)
 
-    def cls_copy(k):
-        return pltpu.make_async_remote_copy(
-            src_ref=blocks.at[c], dst_ref=blocks.at[c], send_sem=cls_s.at[k],
-            recv_sem=cls_r.at[k], device_id=cls_peer(k), device_id_type=MESH)
+    def cls_copy(k, q, slot):
+        return pltpu.make_async_remote_copy(
+            src_ref=blocks.at[c, q], dst_ref=blocks.at[c, q], send_sem=cls_s.at[k, slot],
+            recv_sem=cls_r.at[k, slot], device_id=cls_peer(k), device_id_type=MESH)
 
     def cod_copy(k):
         return pltpu.make_async_remote_copy(
             src_ref=csend.at[lax.rem(r + k, nr)], dst_ref=crecv.at[r], send_sem=cod_s.at[k],
             recv_sem=cod_r.at[k], device_id=row_peer(k), device_id_type=MESH)
 
-    rows = [row_copy(k) for k in range(1, nr)]
-    for d in rows:
+    near = sorted(range(1, nr), key=lambda k: min(k, nr - k))
+    rows = {k: row_copy(k) for k in near}
+    for d in rows.values():
+        d.start()
+    clss = [cls_copy(k, r, 0) for k in range(1, nc)]
+    for d in clss:
         d.start()
 
     quarter = codes_ref[:, pl.ds(pl.multiple_of(c * fq, 128), fq)].astype(f32)
     turned = quarter.T.astype(bf16)
     for j in range(nr):
         csend[j] = turned[j * fb:(j + 1) * fb, :]
-    cods = [cod_copy(k) for k in range(1, nr)]
-    for d in cods:
+    cods = {k: cod_copy(k) for k in near}
+    for d in cods.values():
         d.start()
     crecv[r] = csend[r]
 
-    for d in rows:
-        d.wait_recv()
-    clss = [cls_copy(k) for k in range(1, nc)]
-    for d in clss:
-        d.start()
+    for k in near:
+        rows[k].wait_recv()
+        for m in range(1, nc):
+            d = cls_copy(m, lax.rem(r - k + nr, nr), k)
+            d.start()
+            clss.append(d)
+
+    group = 16
+    steps = [(lax.broadcasted_iota(jnp.int32, (group, Rl), 0) + (g * group + 1)).astype(f32).astype(bf16)
+             for g in range(BINS // group)]
+    zero, one = jnp.zeros((), bf16), jnp.ones((), bf16)
+    for k in [0] + near:
+        if k:
+            cods[k].wait_recv()
+        q = lax.rem(r - k + nr, nr)
+        there = pl.ds(pl.multiple_of(q * Rl, 128), Rl)
+        block = crecv[q].astype(f32)
+        for f in range(fb):
+            row = jnp.broadcast_to(block[f:f + 1, :], (group, Rl)).astype(bf16)
+            for g in range(BINS // group):
+                base = f * BINS + g * group
+                le[base:base + group, there] = jnp.clip(steps[g] - row, zero, one)
     for d in clss:
         d.wait_recv()
 
@@ -130,20 +159,11 @@
     g_all = [g_leaf[2 * n] + g_leaf[2 * n + 1] for n in range(nodes)]
     h_all = [h_leaf[2 * n] + h_leaf[2 * n + 1] for n in range(nodes)]
 
-    for d in cods:
-        d.wait_recv()
-    for q in range(nr):
-        codef[:, q * Rl:(q + 1) * Rl] = crecv[q].astype(f32)
-    above = (lax.broadcasted_iota(jnp.int32, (BINS, R), 0) + 1).astype(f32).astype(bf16)
-    zero, one = jnp.zeros((), bf16), jnp.ones((), bf16)
     width = chunk * BINS
     last = lax.rem(lax.broadcasted_iota(jnp.int32, (CT, width), 1), BINS) == BINS - 1
     best = [None] * nodes
     for i in range(fb // chunk):
-        for j in range(chunk):
-            row = jnp.broadcast_to(codef[i * chunk + j:i * chunk + j + 1, :], (BINS, R)).astype(bf16)
-            le[i % 2, j * BINS:(j + 1) * BINS, :] = jnp.clip(above - row, zero, one)
-        sums = lax.dot_general(wts[...], le[i % 2], (((1,), (1,)), ((), ())),
+        sums = lax.dot_general(wts[...], le[i * width:(i + 1) * width, :], (((1,), (1,)), ((), ())),
                                preferred_element_type=f32)
         for n in range(nodes):
             gl = sums[n * CT:(n + 1) * CT, :]
@@ -156,28 +176,26 @@
             best[n] = gain if best[n] is None else jnp.maximum(best[n], gain)
 
     spot = lax.broadcasted_iota(jnp.int32, (CT, 128), 1)
+    place = lax.rem(lax.broadcasted_iota(jnp.int32, (CT, 128), 0), C) * nodes
     tops = jnp.zeros((CT, 128), f32)
     for n in range(nodes):
         top = jnp.max(best[n], axis=1, keepdims=True)
         den = h_all[n] + REG
         top = (top - g_all[n] * g_all[n] / den) / den
-        tops = jnp.where(spot == n, top, tops)
+        tops = jnp.where(spot == place + n, top, tops)
     for a in range(nc):
-        gsend[a] = tops[a * C:(a + 1) * C, :]
-
-    def g_copy(k):
-        return pltpu.make_async_remote_copy(
-            src_ref=gsend.at[lax.rem(c + k, nc)], dst_ref=grecv.at[k], send_sem=g_s.at[k],
-            recv_sem=g_r.at[k], device_id=cls_peer(k), device_id_type=MESH)
-
-    def h_copy(k):
-        return pltpu.make_async_remote_copy(
-            src_ref=hsend, dst_ref=hrecv.at[k], send_sem=h_s.at[k],
-            recv_sem=h_r.at[k], device_id=row_peer(k), device_id_type=MESH)
-
-    gs_ = [g_copy(k) for k in range(1, nc)]
+        gsend[a] = jnp.sum(tops[a * C:(a + 1) * C, :], axis=0, keepdims=True)
+
+    def g_copy(kc, kr):
+        slot = kc * nr + kr
+        return pltpu.make_async_remote_copy(
+            src_ref=gsend.at[lax.rem(c + kc, nc)], dst_ref=grecv.at[slot], send_sem=g_s.at[slot],
+            recv_sem=g_r.at[slot], device_id=far_peer(kc, kr), device_id_type=MESH)
+
+    gs_ = [g_copy(kc, kr) for kc, kr in far]
     for d in gs_:
         d.start()
+    grecv[0] = gsend[c]
 
     here = pl.ds(pl.multiple_of(r * Rl, 128), Rl)
     tag_own = tags[:, here]
@@ -202,20 +220,25 @@
     hn_ref[...] = nexth[c]
     lv_ref[...] = nextg[c, :, Rl:Rl + leaves]
 
-    top = gsend[c]
-    for k in range(1, nc):
-        gs_[k - 1].wait_recv()
-        top = jnp.maximum(top, grecv[k])
-    hsend[...] = top
-    hs_ = [h_copy(k) for k in range(1, nr)]
-    for d in hs_:
-        d.start()
-    for k in range(1, nr):
-        hs_[k - 1].wait_recv()
-        top = jnp.maximum(top, hrecv[k])
-    bg_ref[...] = top[:, 0:nodes]
-    for d in rows + clss + cods + gs_ + hs_:
+    for d in list(rows.values()) + clss + list(cods.values()):
         d.wait_send()
+    for d in gs_:
+        d.wait_recv()
+    top = jnp.max(grecv[...], axis=0)
+    for i in range(C):
+        line = pltpu.roll(top, (128 - i * nodes) % 128, 1) if i else top
+        bg_ref[i:i + 1, :] = line[:, 0:nodes]
+    for d in gs_:
+        d.wait_send()
+
+
+def put(a, b, c, d, oa, ob, oc, od, sems):
+    copies = [pltpu.make_async_copy(x, y, sems.at[i])
+              for i, (x, y) in enumerate([(a, oa), (b, ob), (c, oc), (d, od)])]
+    for x in copies:
+        x.start()
+    for x in copies:
+        x.wait()
 
 
 def local(codes, split_feature, split_bin, labels, margins):
@@ -230,29 +253,37 @@
     pad = -(-NT * C // 16) * 16
     dma = pltpu.SemaphoreType.DMA
     vmem = pl.BlockSpec(memory_space=pltpu.VMEM)
-    best, leaf, grad, hess = pl.pallas_call(
+    hbm = pl.BlockSpec(memory_space=pltpu.HBM)
+    any_ = pl.BlockSpec(memory_space=pl.ANY)
+    shapes = (jax.ShapeDtypeStruct((C, nodes), f32), jax.ShapeDtypeStruct((C, 2 * nodes), f32),
+              jax.ShapeDtypeStruct((C, Rl), f32), jax.ShapeDtypeStruct((C, Rl), f32))
+    made = pl.pallas_call(
         functools.partial(kernel, (nc, nr, C, Rl, F, NT, chunk)),
-        out_shape=(jax.ShapeDtypeStruct((C, nodes), f32), jax.ShapeDtypeStruct((C, 2 * nodes), f32),
-                   jax.ShapeDtypeStruct((C, Rl), f32), jax.ShapeDtypeStruct((C, Rl), f32)),
-        in_specs=[vmem] * 5,
+        out_shape=shapes,
+        in_specs=[hbm] * 5,
         out_specs=(vmem,) * 4,
         scratch_shapes=[
+            pltpu.VMEM((Rl, F), jnp.int32), pltpu.VMEM((C, NT), jnp.int32), pltpu.VMEM((C, NT), jnp.int32),
+            pltpu.VMEM((1, Rl), jnp.int32), pltpu.VMEM((C, Rl), f32),
             pltpu.VMEM((pad, F), f32), pltpu.VMEM((pad, Rl), f32),
             pltpu.VMEM((nr, fb, Rl), bf16), pltpu.VMEM((nr, fb, Rl), bf16),
             pltpu.VMEM((nc, nr, 2 * C, Rl), f32),
             pltpu.VMEM((CT, R), f32), pltpu.VMEM((CT, R), f32),
-            pltpu.VMEM((fb, R), f32), pltpu.VMEM((2 * nodes * CT, R), bf16),
-            pltpu.VMEM((2, chunk * BINS, R), bf16),
+            pltpu.VMEM((2 * nodes * CT, R), bf16),
+            pltpu.VMEM((fb * BINS, R), bf16),
             pltpu.VMEM((nc, C, Rl + 128), f32), pltpu.VMEM((nc, C, Rl), f32),
-            pltpu.VMEM((nc, C, 128), f32), pltpu.VMEM((nc, C, 128), f32),
-            pltpu.VMEM((C, 128), f32), pltpu.VMEM((nr, C, 128), f32),
-            dma((nr,)), dma((nr,)), dma((nc,)), dma((nc,)), dma((nr,)), dma((nr,)),
-            dma((nc,)), dma((nc,)), dma((nr,)), dma((nr,)),
+            pltpu.VMEM((nc, 1, 128), f32), pltpu.VMEM((nc * nr, 1, 128), f32),
+            dma((5,)), dma((nr,)), dma((nr,)), dma((nc, nr)), dma((nc, nr)), dma((nr,)), dma((nr,)),
+            dma((nc * nr,)), dma((nc * nr,)),
         ],
         compiler_params=pltpu.CompilerParams(
-            collective_id=0, has_side_effects=True, vmem_limit_bytes=48 * 2 ** 20),
+            collective_id=0, has_side_effects=True, vmem_limit_bytes=63 * 2 ** 20),
         name="boost",
     )(codes, split_feature, split_bin, labels.reshape(1, Rl), margins.T)
+    best, leaf, grad, hess = pl.pallas_call(
+        put, out_shape=shapes, in_specs=[any_] * 4, out_specs=(any_,) * 4,
+        scratch_shapes=[dma((4,))], name="put",
+    )(*made)
     return best, leaf, grad.T, hess.T
 
 

time: 31.8 us -> 26.6 us (0.84)
  local copies, waits for them, and re-layouts: 5.61 us -> 0 us
  Pallas kernels: 25.2 us -> 25.8 us
    unnamed x14 -> x0, local copies, waits for them, and re-layouts: 5.61 us -> none
    pallas_call x0 -> x1, Pallas kernels: none -> 1.51 us  [local(): pl.pallas_call(put, out_shape=shapes, in_specs=[any_] * 4, out_specs=(any...]
    pallas_call x1, Pallas kernels: 25.2 us -> 24.3 us  [local(): pl.pallas_call(functools.partial(kernel, (nc, nr, C, Rl, F, NT, chunk)),...]
where the time goes in v2:
time: 26.6 us; the launch traced here: 26.5 us
  Pallas kernels  25.8 us (97%)
  between operations  0.64 us (2%)
    pallas_call x1, Pallas kernels, local(): pl.pallas_call(functools.partial(kernel, (nc, nr, C, Rl, F, NT, chunk)),...  24.3 us
    pallas_call x1, Pallas kernels, local(): pl.pallas_call(put, out_shape=shapes, in_specs=[any_] * 4, out_specs=(any...  1.51 us

profile of v2, /device:TPU:0, one launch (start us, length us, event | category | flops | bytes accessed | tf_op | source)
XLA Modules:
  0.0 26.5 jit_solution(4502750191214591275)
XLA Ops:
  0.6 24.3 %boost.1 = (f32[4,4]{1,0:T(4,128)}, f32[4,8]{1,0:T(4,128)}, f32[4,256]{1,0:T(4,128)}, f32[4,256]{1,0:T(4,128)}) custom-call(s32[256,1024]{1,0:T(8,128)} %codes_in.1, s32[4,7]{1,0:T(4,128)} %sf_in.1, s32[4,7]{1,0:T(4,128)} %sb_in.1, s32[1,256]{1,0:T(1,128)} %bitcast.5, f32[4,256]{1,0:T(4,128)} %bitcast.4), custom_call_target="tpu_custom_call" | custom-call | tf_op jit(solution)/shard_map/boost/pallas_call | solution.py:260
  25.0 1.5 %put.1 = (f32[4,4]{1,0:T(4,128)}, f32[4,8]{1,0:T(4,128)}, f32[4,256]{1,0:T(4,128)}, f32[4,256]{1,0:T(4,128)}) custom-call(f32[4,4]{1,0:T(4,128)} %get-tuple-element.12.a, f32[4,8]{1,0:T(4,128)} %get-tuple-element.13.b, f32[4,256]{1,0:T(4,128)} %get-tuple-element.14.c, f32[4,256]{1,0:T(4,128)} %get-tuple-element.15.d), custom_call_target="tpu_custom_call" | custom-call | tf_op jit(solution)/shard_map/put/pallas_call | solution.py:283

commit v3 on v2

--- a/solution.py
+++ b/solution.py
@@ -27,14 +27,17 @@
     c = lax.axis_index("cls")
     r = lax.axis_index("row")
 
+    cls_at = [jnp.where(c + k >= nc, c + k - nc, c + k) for k in range(nc)]
+    row_at = [jnp.where(r + k >= nr, r + k - nr, r + k) for k in range(nr)]
+
     def row_peer(k):
-        return (c, lax.rem(r + k, nr))
+        return (c, row_at[k])
 
     def cls_peer(k):
-        return (lax.rem(c + k, nc), r)
+        return (cls_at[k], r)
 
     def far_peer(kc, kr):
-        return (lax.rem(c + kc, nc), lax.rem(r + kr, nr))
+        return (cls_at[kc], row_at[kr])
 
     loads = [pltpu.make_async_copy(src, dst, in_s.at[i]) for i, (src, dst) in enumerate(
         [(sf_in, sf_ref), (codes_in, codes_ref), (sb_in, sb_ref), (lab_in, lab_ref), (mar_in, mar_ref)])]
@@ -42,8 +45,10 @@
         d.start()
     barrier = pltpu.get_barrier_semaphore()
     far = [(kc, kr) for kc in range(nc) for kr in range(nr) if kc + kr > 0]
-    for kc, kr in far:
-        pl.semaphore_signal(barrier, inc=1, device_id=far_peer(kc, kr), device_id_type=MESH)
+    for k in range(1, nr):
+        pl.semaphore_signal(barrier, inc=1, device_id=row_peer(k), device_id_type=MESH)
+    for k in range(1, nc):
+        pl.semaphore_signal(barrier, inc=1, device_id=cls_peer(k), device_id_type=MESH)
     for d in loads:
         d.wait()
 
@@ -71,30 +76,29 @@
     blocks[c, r, 0:C, :] = mar_ref[...]
     blocks[c, r, C:2 * C, :] = tag
 
-    pl.semaphore_wait(barrier, nc * nr - 1)
+    pl.semaphore_wait(barrier, nr - 1 + nc - 1)
 
     def row_copy(k):
         return pltpu.make_async_remote_copy(
             src_ref=blocks.at[c, r], dst_ref=blocks.at[c, r], send_sem=row_s.at[k],
             recv_sem=row_r.at[k], device_id=row_peer(k), device_id_type=MESH)
 
-    def cls_copy(k, q, slot):
+    def cls_copy(k, q):
         return pltpu.make_async_remote_copy(
-            src_ref=blocks.at[c, q], dst_ref=blocks.at[c, q], send_sem=cls_s.at[k, slot],
-            recv_sem=cls_r.at[k, slot], device_id=cls_peer(k), device_id_type=MESH)
+            src_ref=blocks.at[c, q], dst_ref=blocks.at[c, q], send_sem=cls_s,
+            recv_sem=cls_r, device_id=cls_peer(k), device_id_type=MESH)
 
     def cod_copy(k):
         return pltpu.make_async_remote_copy(
-            src_ref=csend.at[lax.rem(r + k, nr)], dst_ref=crecv.at[r], send_sem=cod_s.at[k],
+            src_ref=csend.at[row_at[k]], dst_ref=crecv.at[r], send_sem=cod_s.at[k],
             recv_sem=cod_r.at[k], device_id=row_peer(k), device_id_type=MESH)
 
     near = sorted(range(1, nr), key=lambda k: min(k, nr - k))
     rows = {k: row_copy(k) for k in near}
     for d in rows.values():
         d.start()
-    clss = [cls_copy(k, r, 0) for k in range(1, nc)]
-    for d in clss:
-        d.start()
+    for k in range(1, nc):
+        cls_copy(k, r).start()
 
     quarter = codes_ref[:, pl.ds(pl.multiple_of(c * fq, 128), fq)].astype(f32)
     turned = quarter.T.astype(bf16)
@@ -108,9 +112,7 @@
     for k in near:
         rows[k].wait_recv()
         for m in range(1, nc):
-            d = cls_copy(m, lax.rem(r - k + nr, nr), k)
-            d.start()
-            clss.append(d)
+            cls_copy(m, row_at[(nr - k) % nr]).start()
 
     group = 16
     steps = [(lax.broadcasted_iota(jnp.int32, (group, Rl), 0) + (g * group + 1)).astype(f32).astype(bf16)
@@ -119,7 +121,7 @@
     for k in [0] + near:
         if k:
             cods[k].wait_recv()
-        q = lax.rem(r - k + nr, nr)
+        q = row_at[(nr - k) % nr]
         there = pl.ds(pl.multiple_of(q * Rl, 128), Rl)
         block = crecv[q].astype(f32)
         for f in range(fb):
@@ -127,8 +129,11 @@
             for g in range(BINS // group):
                 base = f * BINS + g * group
                 le[base:base + group, there] = jnp.clip(steps[g] - row, zero, one)
-    for d in clss:
-        d.wait_recv()
+    others = blocks.at[pl.ds(0, nc - 1)]
+    gathered = pltpu.make_async_remote_copy(
+        src_ref=others, dst_ref=others, send_sem=cls_s, recv_sem=cls_r,
+        device_id=cls_peer(1), device_id_type=MESH)
+    gathered.wait_recv()
 
     for a in range(nc):
         for q in range(nr):
@@ -189,8 +194,8 @@
     def g_copy(kc, kr):
         slot = kc * nr + kr
         return pltpu.make_async_remote_copy(
-            src_ref=gsend.at[lax.rem(c + kc, nc)], dst_ref=grecv.at[slot], send_sem=g_s.at[slot],
-            recv_sem=g_r.at[slot], device_id=far_peer(kc, kr), device_id_type=MESH)
+            src_ref=gsend.at[cls_at[kc]], dst_ref=grecv.at[slot], send_sem=g_s,
+            recv_sem=g_r, device_id=far_peer(kc, kr), device_id_type=MESH)
 
     gs_ = [g_copy(kc, kr) for kc, kr in far]
     for d in gs_:
@@ -220,16 +225,19 @@
     hn_ref[...] = nexth[c]
     lv_ref[...] = nextg[c, :, Rl:Rl + leaves]
 
-    for d in list(rows.values()) + clss + list(cods.values()):
+    gathered.wait_send()
+    for d in list(rows.values()) + list(cods.values()):
         d.wait_send()
-    for d in gs_:
-        d.wait_recv()
+    every = grecv.at[pl.ds(1, nc * nr - 1)]
+    whole = pltpu.make_async_remote_copy(
+        src_ref=every, dst_ref=every, send_sem=g_s, recv_sem=g_r,
+        device_id=far_peer(*far[0]), device_id_type=MESH)
+    whole.wait_recv()
     top = jnp.max(grecv[...], axis=0)
     for i in range(C):
         line = pltpu.roll(top, (128 - i * nodes) % 128, 1) if i else top
         bg_ref[i:i + 1, :] = line[:, 0:nodes]
-    for d in gs_:
-        d.wait_send()
+    whole.wait_send()
 
 
 def put(a, b, c, d, oa, ob, oc, od, sems):
@@ -273,15 +281,15 @@
             pltpu.VMEM((fb * BINS, R), bf16),
             pltpu.VMEM((nc, C, Rl + 128), f32), pltpu.VMEM((nc, C, Rl), f32),
             pltpu.VMEM((nc, 1, 128), f32), pltpu.VMEM((nc * nr, 1, 128), f32),
-            dma((5,)), dma((nr,)), dma((nr,)), dma((nc, nr)), dma((nc, nr)), dma((nr,)), dma((nr,)),
-            dma((nc * nr,)), dma((nc * nr,)),
+            dma((5,)), dma((nr,)), dma((nr,)), dma(()), dma(()), dma((nr,)), dma((nr,)),
+            dma(()), dma(()),
         ],
         compiler_params=pltpu.CompilerParams(
             collective_id=0, has_side_effects=True, vmem_limit_bytes=63 * 2 ** 20),
         name="boost",
     )(codes, split_feature, split_bin, labels.reshape(1, Rl), margins.T)
     best, leaf, grad, hess = pl.pallas_call(
-        put, out_shape=shapes, in_specs=[any_] * 4, out_specs=(any_,) * 4,
+        put, out_shape=shapes, in_specs=[vmem] * 4, out_specs=(any_,) * 4,
         scratch_shapes=[dma((4,))], name="put",
     )(*made)
     return best, leaf, grad.T, hess.T

time: 26.6 us -> 23.5 us (0.88)
  Pallas kernels: 25.8 us -> 22.7 us
    pallas_call x1, Pallas kernels: 24.3 us -> 21.4 us  [local(): pl.pallas_call(functools.partial(kernel, (nc, nr, C, Rl, F, NT, chunk)),...]
where the time goes in v3:
time: 23.5 us; the launch traced here: 23.4 us
  Pallas kernels  22.7 us (97%)
  between operations  0.64 us (3%)
    pallas_call x1, Pallas kernels, local(): pl.pallas_call(functools.partial(kernel, (nc, nr, C, Rl, F, NT, chunk)),...  21.4 us
    pallas_call x1, Pallas kernels, local(): pl.pallas_call(put, out_shape=shapes, in_specs=[vmem] * 4, out_specs=(any...  1.33 us

profile of v3, /device:TPU:0, one launch (start us, length us, event | category | flops | bytes accessed | tf_op | source)
XLA Modules:
  0.0 23.4 jit_solution(17197390501423679674)
XLA Ops:
  0.6 21.4 %boost.1 = (f32[4,4]{1,0:T(4,128)}, f32[4,8]{1,0:T(4,128)}, f32[4,256]{1,0:T(4,128)}, f32[4,256]{1,0:T(4,128)}) custom-call(s32[256,1024]{1,0:T(8,128)} %codes_in.1, s32[4,7]{1,0:T(4,128)} %sf_in.1, s32[4,7]{1,0:T(4,128)} %sb_in.1, s32[1,256]{1,0:T(1,128)} %bitcast.5, f32[4,256]{1,0:T(4,128)} %bitcast.4), custom_call_target="tpu_custom_call" | custom-call | tf_op jit(solution)/shard_map/boost/pallas_call | solution.py:268
  22.0 1.3 %put.1 = (f32[4,4]{1,0:T(4,128)}, f32[4,8]{1,0:T(4,128)}, f32[4,256]{1,0:T(4,128)}, f32[4,256]{1,0:T(4,128)}) custom-call(f32[4,4]{1,0:T(4,128)} %get-tuple-element.12.a, f32[4,8]{1,0:T(4,128)} %get-tuple-element.13.b, f32[4,256]{1,0:T(4,128)} %get-tuple-element.14.c, f32[4,256]{1,0:T(4,128)} %get-tuple-element.15.d), custom_call_target="tpu_custom_call" | custom-call | tf_op jit(solution)/shard_map/put/pallas_call | solution.py:291

commit v4 on v3

--- a/solution.py
+++ b/solution.py
@@ -285,12 +285,14 @@
             dma(()), dma(()),
         ],
         compiler_params=pltpu.CompilerParams(
-            collective_id=0, has_side_effects=True, vmem_limit_bytes=63 * 2 ** 20),
+            collective_id=0, has_side_effects=True, vmem_limit_bytes=32 * 2 ** 20),
         name="boost",
-    )(codes, split_feature, split_bin, labels.reshape(1, Rl), margins.T)
+    )(*[pltpu.with_memory_space_constraint(x, pltpu.HBM)
+        for x in (codes, split_feature, split_bin, labels.reshape(1, Rl), margins.T)])
     best, leaf, grad, hess = pl.pallas_call(
-        put, out_shape=shapes, in_specs=[vmem] * 4, out_specs=(any_,) * 4,
+        put, out_shape=shapes, in_specs=[vmem] * 4, out_specs=(hbm,) * 4,
         scratch_shapes=[dma((4,))], name="put",
+        compiler_params=pltpu.CompilerParams(vmem_limit_bytes=2 ** 20),
     )(*made)
     return best, leaf, grad.T, hess.T
 

time: 23.5 us -> 22.2 us (0.945)
  Pallas kernels: 22.7 us -> 21.4 us
    pallas_call x1, Pallas kernels: 1.33 us -> 0.64 us  [local(): pl.pallas_call(put, out_shape=shapes, in_specs=[vmem] * 4, out_specs=(hbm...]
    pallas_call x1, Pallas kernels: 21.4 us -> 20.8 us  [local(): pl.pallas_call(functools.partial(kernel, (nc, nr, C, Rl, F, NT, chunk)),...]
where the time goes in v4:
time: 22.2 us; the launch traced here: 22.1 us
  Pallas kernels  21.4 us (96%)
  between operations  0.64 us (3%)
    pallas_call x1, Pallas kernels, local(): pl.pallas_call(functools.partial(kernel, (nc, nr, C, Rl, F, NT, chunk)),...  20.8 us
    pallas_call x1, Pallas kernels, local(): pl.pallas_call(put, out_shape=shapes, in_specs=[vmem] * 4, out_specs=(hbm...  0.64 us

profile of v4, /device:TPU:0, one launch (start us, length us, event | category | flops | bytes accessed | tf_op | source)
XLA Modules:
  0.0 22.1 jit_solution(11745951435868758225)
XLA Ops:
  0.6 20.8 %boost.1 = (f32[4,4]{1,0:T(4,128)S(1)}, f32[4,8]{1,0:T(4,128)S(1)}, f32[4,256]{1,0:T(4,128)S(1)}, f32[4,256]{1,0:T(4,128)S(1)}) custom-call(s32[256,1024]{1,0:T(8,128)} %codes_in.1, s32[4,7]{1,0:T(4,128)} %sf_in.1, s32[4,7]{1,0:T(4,128)} %sb_in.1, s32[1,256]{1,0:T(1,128)} %bitcast.5, f32[4,256]{1,0:T(4,128)} %bitcast.4), custom_call_target="tpu_custom_call" | custom-call | tf_op jit(solution)/shard_map/boost/pallas_call | solution.py:268
  21.4 0.6 %put.1 = (f32[4,4]{1,0:T(4,128)}, f32[4,8]{1,0:T(4,128)}, f32[4,256]{1,0:T(4,128)}, f32[4,256]{1,0:T(4,128)}) custom-call(f32[4,4]{1,0:T(4,128)S(1)} %get-tuple-element.12.a, f32[4,8]{1,0:T(4,128)S(1)} %get-tuple-element.13.b, f32[4,256]{1,0:T(4,128)S(1)} %get-tuple-element.14.c, f32[4,256]{1,0:T(4,128)S(1)} %get-tuple-element.15.d), custom_call_target="tpu_custom_call" | custom-call | tf_op jit(solution)/shard_map/put/pallas_call | solution.py:292

commit v5 on v4

--- a/solution.py
+++ b/solution.py
@@ -49,13 +49,14 @@
         pl.semaphore_signal(barrier, inc=1, device_id=row_peer(k), device_id_type=MESH)
     for k in range(1, nc):
         pl.semaphore_signal(barrier, inc=1, device_id=cls_peer(k), device_id_type=MESH)
-    for d in loads:
-        d.wait()
+    loads[0].wait()
 
     lane = lax.broadcasted_iota(jnp.int32, (C, F), 1)
     sel[...] = jnp.zeros_like(sel)
     for n in range(NT):
         sel[n * C:(n + 1) * C, :] = jnp.where(lane == sf_ref[:, n:n + 1], 1.0, 0.0).astype(f32)
+    for d in loads[1:]:
+        d.wait()
     low = codes_ref[...].astype(f32).astype(bf16)
     picked[...] = lax.dot_general(sel[...].astype(bf16), low, (((1,), (1,)), ((), ())),
                                   preferred_element_type=f32)
@@ -197,7 +198,7 @@
             src_ref=gsend.at[cls_at[kc]], dst_ref=grecv.at[slot], send_sem=g_s,
             recv_sem=g_r, device_id=far_peer(kc, kr), device_id_type=MESH)
 
-    gs_ = [g_copy(kc, kr) for kc, kr in far]
+    gs_ = [g_copy(kc, kr) for kc, kr in sorted(far, key=lambda p: (-min(p[1], nr - p[1]), -p[0]))]
     for d in gs_:
         d.start()
     grecv[0] = gsend[c]
@@ -256,7 +257,7 @@
     nodes = (NT + 1) // 2
     CT, R = C * nc, Rl * nr
     fb = F // (nc * nr)
-    chunk = min(4, fb)
+    chunk = min(8, fb)
     f32, bf16 = jnp.float32, jnp.bfloat16
     pad = -(-NT * C // 16) * 16
     dma = pltpu.SemaphoreType.DMA

time: 22.2 us -> 22.2 us (level)
  no operation moved by 1% of the time
where the time goes in v5:
time: 22.2 us; the launch traced here: 22 us
  Pallas kernels  21.4 us (96%)
  between operations  0.64 us (3%)
    pallas_call x1, Pallas kernels, local(): pl.pallas_call(functools.partial(kernel, (nc, nr, C, Rl, F, NT, chunk)),...  20.7 us
    pallas_call x1, Pallas kernels, local(): pl.pallas_call(put, out_shape=shapes, in_specs=[vmem] * 4, out_specs=(hbm...  0.64 us

profile of v5, /device:TPU:0, one launch (start us, length us, event | category | flops | bytes accessed | tf_op | source)
XLA Modules:
  0.0 22.0 jit_solution(3111609723985545889)
XLA Ops:
  0.6 20.7 %boost.1 = (f32[4,4]{1,0:T(4,128)S(1)}, f32[4,8]{1,0:T(4,128)S(1)}, f32[4,256]{1,0:T(4,128)S(1)}, f32[4,256]{1,0:T(4,128)S(1)}) custom-call(s32[256,1024]{1,0:T(8,128)} %codes_in.1, s32[4,7]{1,0:T(4,128)} %sf_in.1, s32[4,7]{1,0:T(4,128)} %sb_in.1, s32[1,256]{1,0:T(1,128)} %bitcast.5, f32[4,256]{1,0:T(4,128)} %bitcast.4), custom_call_target="tpu_custom_call" | custom-call | tf_op jit(solution)/shard_map/boost/pallas_call | solution.py:269
  21.4 0.6 %put.1 = (f32[4,4]{1,0:T(4,128)}, f32[4,8]{1,0:T(4,128)}, f32[4,256]{1,0:T(4,128)}, f32[4,256]{1,0:T(4,128)}) custom-call(f32[4,4]{1,0:T(4,128)S(1)} %get-tuple-element.12.a, f32[4,8]{1,0:T(4,128)S(1)} %get-tuple-element.13.b, f32[4,256]{1,0:T(4,128)S(1)} %get-tuple-element.14.c, f32[4,256]{1,0:T(4,128)S(1)} %get-tuple-element.15.d), custom_call_target="tpu_custom_call" | custom-call | tf_op jit(solution)/shard_map/put/pallas_call | solution.py:293
